TPU v7x, 32 devices: a whole 2x2x4 slice. The times are simulated.
32 devices in a mesh: section: 2 (over core), fsdp: 4 (over z), dp: 4 (over y, x).
Axes of the slice: x: 2, y: 2, z: 4, core: 2. Of those that a mesh axis runs over, the one named last changes fastest.
Arguments:
- tokens: bfloat16 [1, 16, 128, 1024], P(None, ('fsdp', 'dp')), may hold values from -6 to 6
- segments: int32 [1, 16, 128], P(None, ('fsdp', 'dp')), may hold values from 0 to 3, never falling along the last dimension, each value on 1 to 64 neighbouring positions
- cotangent: float32 [1, 16, 128, 1024], P(None, ('fsdp', 'dp')), may hold values from -6 to 6
- norm_gains: bfloat16 [2, 2, 1024], P('section', None, 'fsdp'), may hold values from 0.5 to 1.5
- proj_weight: bfloat16 [2, 1024, 3072], P('section', 'fsdp'), may hold values from -0.1875 to 0.1875
- rate_weight: bfloat16 [2, 1024, 8], P('section', 'fsdp'), may hold values from -0.1875 to 0.1875
- out_weight: bfloat16 [2, 1024, 1024], P('section', 'fsdp'), may hold values from -0.375 to 0.375
- up_weight: bfloat16 [2, 1024, 5632], P('section', 'fsdp'), may hold values from -0.1875 to 0.1875
- down_weight: bfloat16 [2, 1024, 2816], P('section', 'fsdp'), may hold values from -0.21875 to 0.21875
- conv_kernels: float32 [2, 4, 2048], P('section'), may hold values from -3 to 3
- head_params: float32 [2, 2, 4], P('section'), may hold values from -2.5 to 0.5
- out_gain: float32 [2, 256], P('section'), may hold values from 0.5 to 1.5
Outputs:
- section_output: bfloat16 [2, 1, 16, 128, 1024], P('section', None, ('fsdp', 'dp'))
- input_grad: float32 [2, 1, 16, 128, 1024], P('section', None, ('fsdp', 'dp'))
- gains_grad: float32 [2, 2, 1024], P('section', None, 'fsdp')
- proj_grad: float32 [2, 1024, 3072], P('section', 'fsdp')
- rate_grad: float32 [2, 1024, 8], P('section', 'fsdp')
- out_grad: float32 [2, 1024, 1024], P('section', 'fsdp')
- up_grad: float32 [2, 1024, 5632], P('section', 'fsdp')
- down_grad: float32 [2, 1024, 2816], P('section', 'fsdp')
- kernel_grad: float32 [2, 4, 2048], P('section')
- head_grad: float32 [2, 2, 4], P('section')
- out_gain_grad: float32 [2, 256], P('section')
Inputs may be any that keep to these rules, and one draw needn't show every extreme that they name: `segments`: within each sequence the numbers never fall, every one of 0 .. 3 occurs, and each document holds 1 to 64 positions, one exactly 64.
All inputs are finite; a program needn't handle non-finite values.
Results may differ from a plain program's by a relative error of at most 0.034.
Values may be sent and summed in bfloat16 or wider, within the bound.
A program may use at most 256 MiB of HBM per device.

v0:
```python
from functools import partial
import jax
import jax.numpy as jnp
from jax import lax
from jax.sharding import PartitionSpec as P

SPAN = 64
highest = lax.Precision.HIGHEST
reset_level = -30.0


def passed_along(value, axis, steps):
    count = lax.axis_size(axis)
    leading, last = (max(0, -steps), min(count, count - steps))
    return lax.ppermute(value, axis, [(source, source + steps) for source in range(leading, last)])


def rms_gain(values, gain_vec):
    return values * lax.rsqrt(jnp.mean(values * values, -1, keepdims=True) + 1e-06) * gain_vec


def swiglu(joined):
    half_width = joined.shape[-1] // 2
    return jax.nn.silu(joined[..., :half_width]) * joined[..., half_width:]


def short_conv(raw_input, kernel, segment):
    length = raw_input.shape[1]
    tap_count = kernel.shape[0]
    total = raw_input * kernel[tap_count - 1]
    for offset in range(1, tap_count):
        shifted = jnp.pad(raw_input, ((0, 0), (offset, 0), (0, 0)))[:, :length]
        earlier = jnp.pad(segment, ((0, 0), (offset, 0)), constant_values=-1)[:, :length]
        total = (
            total
            + jnp.where((earlier == segment)[..., None], shifted, 0.0)
            * kernel[tap_count - 1 - offset]
        )
    return jax.nn.silu(total)


def delta_rule(queries, key_rows, value_rows, beta_gate, decays, block_len):
    batch_size, head_count, length, key_dim = queries.shape
    value_dim = value_rows.shape[-1]
    block_count = length // block_len

    def to_blocks(array):
        return array.reshape(array.shape[:2] + (block_count, block_len) + array.shape[3:])

    queries = to_blocks(queries)
    key_rows = to_blocks(key_rows)
    value_rows = to_blocks(value_rows)
    beta_gate = to_blocks(beta_gate)
    levels = jnp.cumsum(to_blocks(decays), axis=-1)
    places = jnp.arange(block_len)
    lower_mask = places[:, None] >= places[None, :]
    strict_mask = places[:, None] > places[None, :]
    spread = jnp.exp(jnp.where(lower_mask, levels[..., :, None] - levels[..., None, :], -1e30))
    beta_keys = key_rows * beta_gate[..., None]
    key_inner = jnp.einsum("bhncd,bhnmd->bhncm", beta_keys, key_rows, precision=highest) * spread
    system = jnp.where(strict_mask, key_inner, 0.0)
    right_side = jnp.concatenate(
        [beta_keys * jnp.exp(levels)[..., None], value_rows * beta_gate[..., None]], -1
    )
    solved = lax.linalg.triangular_solve(
        system, right_side, left_side=True, lower=True, unit_diagonal=True
    )
    solved_keys = solved[..., :key_dim]
    solved_values = solved[..., key_dim:]
    scores = jnp.einsum("bhncd,bhnmd->bhncm", queries, key_rows, precision=highest) * spread
    fading = queries * jnp.exp(levels)[..., None]
    final_level = levels[..., -1:]
    carried = key_rows * jnp.exp(final_level - levels)[..., None]

    def advance(memory, pieces):
        fading_part, keys_part, values_part, scores_part, carried_part, final_part = pieces
        update = values_part - jnp.einsum("bhcd,bhde->bhce", keys_part, memory, precision=highest)
        output = jnp.einsum("bhcd,bhde->bhce", fading_part, memory, precision=highest) + jnp.einsum(
            "bhcm,bhme->bhce", scores_part, update, precision=highest
        )
        memory = memory * jnp.exp(final_part)[..., None] + jnp.einsum(
            "bhcd,bhce->bhde", carried_part, update, precision=highest
        )
        return (memory, output)

    pieces = tuple(
        (
            jnp.moveaxis(array, 2, 0)
            for array in (fading, solved_keys, solved_values, scores, carried, final_level)
        )
    )
    initial = jnp.zeros((batch_size, head_count, key_dim, value_dim), queries.dtype)
    _, outputs = lax.scan(advance, initial, pieces)
    return jnp.moveaxis(outputs, 0, 2).reshape(batch_size, head_count, length, value_dim)


def token_mixer(projected, rate_logits, kernel, head_params, out_gain, segment):
    batch_size, length, _ = projected.shape
    head_count = head_params.shape[1]
    value_dim = out_gain.shape[0]
    channels = kernel.shape[1]
    key_width = (channels - head_count * value_dim) // 2
    key_dim = key_width // head_count
    mixed = short_conv(projected[..., :channels], kernel, segment)

    def heads_of(array, size):
        return jnp.moveaxis(array.reshape(batch_size, length, head_count, size), 2, 1)

    queries = heads_of(mixed[..., :key_width], key_dim)
    key_rows = heads_of(mixed[..., key_width : 2 * key_width], key_dim)
    value_rows = heads_of(mixed[..., 2 * key_width :], value_dim)
    queries = (
        queries
        * lax.rsqrt(jnp.sum(queries * queries, -1, keepdims=True) + 1e-06)
        * key_dim ** (-0.5)
    )
    key_rows = key_rows * lax.rsqrt(jnp.sum(key_rows * key_rows, -1, keepdims=True) + 1e-06)
    beta_gate = jax.nn.sigmoid(jnp.moveaxis(rate_logits[..., head_count:], 2, 1))
    decays = -jnp.exp(head_params[0])[:, None] * jax.nn.softplus(
        jnp.moveaxis(rate_logits[..., :head_count], 2, 1) + head_params[1][:, None]
    )
    earlier = jnp.pad(segment, ((0, 0), (1, 0)), constant_values=-1)[:, :length]
    decays = jnp.where((earlier != segment)[:, None, :], reset_level, decays)
    output = delta_rule(queries, key_rows, value_rows, beta_gate, decays, SPAN)
    output = output * lax.rsqrt(jnp.mean(output * output, -1, keepdims=True) + 1e-05) * out_gain
    gating = heads_of(projected[..., channels:], value_dim)
    return jnp.moveaxis(output * jax.nn.silu(gating), 1, 2).reshape(
        batch_size, length, head_count * value_dim
    )


def last_contract(left, right):
    return lax.dot_general(
        left, right, (((2,), (1,)), ((), ())), preferred_element_type=jnp.float32
    )


def layer_forward(entering, segment, weights, small_params):
    norm_gains, proj_weight, rate_weight, out_weight, up_weight, down_weight = weights
    kernel, head_params, out_gain = small_params
    widened = entering.astype(jnp.float32)
    normed_one, norm_one_back = jax.vjp(rms_gain, widened, norm_gains[0].astype(jnp.float32))
    hidden_one = normed_one.astype(jnp.bfloat16)
    projected = jnp.dot(hidden_one, proj_weight, preferred_element_type=jnp.float32)
    rate_logits = jnp.dot(hidden_one, rate_weight, preferred_element_type=jnp.float32)
    mixed_out, mixer_back = jax.vjp(
        partial(token_mixer, segment=segment), projected, rate_logits, kernel, head_params, out_gain
    )
    mixed_half = mixed_out.astype(jnp.bfloat16)
    stream = widened + last_contract(mixed_half, out_weight)
    normed_two, norm_two_back = jax.vjp(rms_gain, stream, norm_gains[1].astype(jnp.float32))
    hidden_two = normed_two.astype(jnp.bfloat16)
    gate_up = jnp.dot(hidden_two, up_weight, preferred_element_type=jnp.float32)
    activated, act_back = jax.vjp(swiglu, gate_up)
    act_half = activated.astype(jnp.bfloat16)
    layer_out = (stream + last_contract(act_half, down_weight)).astype(jnp.bfloat16)
    residuals = (
        norm_one_back,
        hidden_one,
        mixer_back,
        mixed_half,
        norm_two_back,
        hidden_two,
        act_back,
        act_half,
    )
    return (layer_out, residuals)


def layer_backward(cotangent_in, residuals, weights):
    norm_gains, proj_weight, rate_weight, out_weight, up_weight, down_weight = weights
    (
        norm_one_back,
        hidden_one,
        mixer_back,
        mixed_half,
        norm_two_back,
        hidden_two,
        act_back,
        act_half,
    ) = residuals
    dout_half = cotangent_in.astype(jnp.bfloat16)
    (gate_up_grad,) = act_back(jnp.dot(dout_half, down_weight, preferred_element_type=jnp.float32))
    gate_up_cot = gate_up_grad.astype(jnp.bfloat16)
    stream_grad, gain_two = norm_two_back(last_contract(gate_up_cot, up_weight))
    stream_grad = cotangent_in + stream_grad
    branch_cot = stream_grad.astype(jnp.bfloat16)
    proj_grad, rate_grad, kernel_grad, head_grad, out_gain_grad = mixer_back(
        jnp.dot(branch_cot, out_weight, preferred_element_type=jnp.float32)
    )
    proj_cot = proj_grad.astype(jnp.bfloat16)
    rate_cot = rate_grad.astype(jnp.bfloat16)
    hidden_grad = last_contract(proj_cot, proj_weight) + last_contract(rate_cot, rate_weight)
    entry_grad, gain_one = norm_one_back(hidden_grad)
    pairs = (
        hidden_one,
        proj_cot,
        rate_cot,
        mixed_half,
        branch_cot,
        hidden_two,
        gate_up_cot,
        act_half,
        dout_half,
    )
    return (
        stream_grad + entry_grad,
        pairs,
        (kernel_grad, head_grad, out_gain_grad),
        jnp.stack([gain_one, gain_two]),
    )


def weight_terms(pairs, gain_sum, start, count):
    flattened = [member.reshape(-1, member.shape[-1]) for member in pairs]
    (
        hidden_one,
        proj_cot,
        rate_cot,
        mixed_half,
        branch_cot,
        hidden_two,
        gate_up_cot,
        act_half,
        dout_half,
    ) = flattened

    def product(left, right):
        return lax.dot_general(
            left, right, (((0,), (0,)), ((), ())), preferred_element_type=jnp.float32
        )

    return jnp.concatenate(
        [
            product(hidden_one, proj_cot),
            product(hidden_one, rate_cot),
            product(branch_cot, mixed_half),
            product(hidden_two, gate_up_cot),
            product(dout_half, act_half),
            gain_sum.T,
        ],
        1,
    )


def split_term(total, widths):
    pieces = []
    column = 0
    for width in widths:
        pieces.append(total[..., column : column + width])
        column = column + width
    return pieces


def pass_forward(layer_out):
    return passed_along(layer_out, "section", 1)


def pass_backward(entry_grad):
    return passed_along(entry_grad.astype(jnp.bfloat16), "section", -1).astype(entry_grad.dtype)


def shards(
    tokens,
    segments,
    cotangent,
    norm_gains,
    proj_weight,
    rate_weight,
    out_weight,
    up_weight,
    down_weight,
    conv_kernels,
    head_params,
    out_gain,
):
    first_section = lax.axis_index("section") == 0
    weights = (
        lax.all_gather(norm_gains[0], "fsdp", axis=1, tiled=True),
        lax.all_gather(proj_weight[0], "fsdp", axis=0, tiled=True),
        lax.all_gather(rate_weight[0], "fsdp", axis=0, tiled=True),
        lax.all_gather(out_weight[0], "fsdp", axis=0, tiled=True),
        lax.all_gather(up_weight[0], "fsdp", axis=0, tiled=True),
        lax.all_gather(down_weight[0], "fsdp", axis=0, tiled=True),
    )
    small_params = (conv_kernels[0], head_params[0], out_gain[0])
    batches = tokens.shape[0]
    records = []
    results = []
    for forward_step in range(batches + 1):
        ahead_batch = min(forward_step, batches - 1)
        behind = max(forward_step - 1, 0)
        segment = jnp.where(first_section, segments[ahead_batch], segments[behind])
        if forward_step == 0:
            entering = tokens[0]
        else:
            entering = jnp.where(first_section, tokens[ahead_batch], pass_forward(results[-1]))
        produced, residuals = layer_forward(entering, segment, weights, small_params)
        records.append(residuals)
        results.append(produced)
    incoming = []
    kept_pairs = []
    small_list = []
    gain_list = []
    for backward_step in range(batches + 1):
        if backward_step < batches:
            own_cot = cotangent[batches - 1 - backward_step]
        else:
            own_cot = jnp.zeros_like(cotangent[0])
        if backward_step == 0:
            upstream = jnp.zeros_like(own_cot)
        else:
            upstream = pass_backward(incoming[-1])
        dout_full = jnp.where(first_section, upstream, own_cot)
        entry_grad, pairs, small_grads, gains_step = layer_backward(
            dout_full, records[batches - backward_step], weights
        )
        incoming.append(entry_grad)
        kept_pairs.append(pairs)
        small_list.append(small_grads)
        gain_list.append(gains_step)
    pairs_all = tuple((jnp.concatenate([member[i] for member in kept_pairs], 1) for i in range(9)))
    gain_sum = sum(gain_list)
    small_sum = tuple((sum((member[i] for member in small_list)) for i in range(3)))
    section_output = jnp.stack([jnp.where(first_section, results[0], results[1])])[None]
    input_grad = jnp.stack([jnp.where(first_section, incoming[batches], incoming[batches - 1])])[
        None
    ]
    own_rows = proj_weight.shape[1]
    term_of = partial(weight_terms, pairs_all, gain_sum)
    totals = lax.psum_scatter(
        term_of(jnp.int32(0), own_rows * lax.axis_size("fsdp")).astype(jnp.bfloat16),
        "fsdp",
        scatter_dimension=0,
        tiled=True,
    ).astype(jnp.float32)
    totals = lax.psum(totals.astype(jnp.bfloat16), "dp").astype(jnp.float32)
    kernel_grad, head_grad, out_gain_grad = lax.psum(
        (small_sum[0], small_sum[1], small_sum[2]), ("fsdp", "dp")
    )
    widths = [
        proj_weight.shape[2],
        rate_weight.shape[2],
        out_weight.shape[2],
        up_weight.shape[2],
        down_weight.shape[2],
        2,
    ]
    pieces = split_term(totals, widths)
    return (
        section_output,
        input_grad,
        pieces[5].T[None],
        pieces[0][None],
        pieces[1][None],
        pieces[2][None],
        pieces[3][None],
        pieces[4][None],
        kernel_grad[None],
        head_grad[None],
        out_gain_grad[None],
    )


def solution(mesh):
    return jax.shard_map(
        shards,
        mesh=mesh,
        in_specs=(
            P(None, ("fsdp", "dp"), None, None),
            P(None, ("fsdp", "dp"), None),
            P(None, ("fsdp", "dp"), None, None),
            P("section", None, "fsdp"),
            P("section", "fsdp", None),
            P("section", "fsdp", None),
            P("section", "fsdp", None),
            P("section", "fsdp", None),
            P("section", "fsdp", None),
            P("section", None, None),
            P("section", None, None),
            P("section", None),
        ),
        out_specs=(
            P("section", None, ("fsdp", "dp"), None, None),
            P("section", None, ("fsdp", "dp"), None, None),
            P("section", None, "fsdp"),
            P("section", "fsdp", None),
            P("section", "fsdp", None),
            P("section", "fsdp", None),
            P("section", "fsdp", None),
            P("section", "fsdp", None),
            P("section", None, None),
            P("section", None, None),
            P("section", None),
        ),
        check_vma=False,
    )
```

profile of v0, /device:TPU:0, one launch (start us, length us, event | category | flops | bytes accessed | tf_op | source)
XLA Modules:
  0.0 1455.5 jit_solution(11192671535240137623)
XLA Ops:
  10.3 12.7 all-gather
  23.2 13.7 all-gather.1
  41.3 86.5 %all-gather.11.cloned.1.call-done = bf16[1,1024,3072]{2,1,0:T(8,128)(2,1)} async-done(((bf16[1,256,3072]{2,1,0:T(8,128)(2,1)}), bf16[1,1024,3072]{2,1,0:T(8,128)(2,1)}) %all-gather.11.cloned.1.call-update) | async-done | bytes 6291472 | tf_op jit(solution)/shard_map/all_gather | solution.py:280
  127.9 3.8 fusion.194
  141.4 39.3 %custom-call.16 = f32[1,4,2,1,64,64]{4,5,3,2,1,0:T(8,128)S(1)} custom-call(f32[1,4,2,1,64,64]{5,4,3,2,1,0:T(8,128)S(1)} %fusion.409), custom_call_target="InvertDiagBlocksLowerTriangular" | custom-call | tf_op jit(solution)/shard_map/jvp()/triangular_solve/custom-call.1 | solution.py:65
  185.2 7.1 while.96
  199.1 2.6 multiply_reduce_fusion.16
  201.8 173.0 %all-gather.15.cloned.1.call-done = bf16[1,1024,5632]{2,1,0:T(8,128)(2,1)} async-done(((bf16[1,256,5632]{2,1,0:T(8,128)(2,1)}), bf16[1,1024,5632]{2,1,0:T(8,128)(2,1)}) %all-gather.15.cloned.1.call-update) | async-done | bytes 11534352 | tf_op jit(solution)/shard_map/all_gather | solution.py:283
  374.8 6.0 fusion.166
  382.8 98.3 %all-gather.17.cloned.1.call-done = bf16[1,1024,2816]{2,1,0:T(8,128)(2,1)} async-done(((bf16[1,256,2816]{2,1,0:T(8,128)(2,1)}), bf16[1,1024,2816]{2,1,0:T(8,128)(2,1)}) %all-gather.17.cloned.1.call-update) | async-done | bytes 5767184 | tf_op jit(solution)/shard_map/all_gather | solution.py:284
  481.2 4.6 fusion.242
  487.7 3.9 copy.525
  493.1 3.8 fusion.197
  508.6 2.2 reshape.2341
  515.8 40.7 %custom-call.17 = f32[1,4,2,1,64,64]{4,5,3,2,1,0:T(8,128)} custom-call(f32[1,4,2,1,64,64]{5,4,3,2,1,0:T(8,128)} %fusion.397), custom_call_target="InvertDiagBlocksLowerTriangular" | custom-call | tf_op jit(solution)/shard_map/jvp()/triangular_solve/custom-call.1 | solution.py:65
  576.0 11.5 while.97
  596.9 2.7 multiply_reduce_fusion.14
  599.8 6.1 fusion.169
  606.0 2.3 fusion.437
  608.5 4.4 fusion.349
  622.0 26.4 %while.98 = (s32[]{:T(128)}, f32[1,4,128,256]{2,3,1,0:T(8,128)S(1)}, f32[2,1,4,64,128]{4,3,0,2,1:T(8,128)}, f32[2,1,4,64,128]{4,3,2,1,0:T(8,128)}, f32[2,1,4,64,...) while((s32[]{:T(128)}, ...), condition=%wide.region_20.23_spmd.clone, body=%wide.region_18.22_spmd.clone.sunk | while | flops 706019328 | bytes 25702096 | solution.py:93
  648.4 3.2 fusion.296
  651.7 2.8 convolution_bitcast_fusion.17
  667.7 2.4 fusion.539
  678.4 2.6 multiply_select_fusion.3
  690.0 2.7 fusion.275
  693.7 2.2 fusion.174
  702.5 4.9 fusion.436
  708.3 3.7 fusion.158
  720.8 19.1 %while.99 = (s32[]{:T(128)}, f32[1,4,128,256]{2,3,1,0:T(8,128)S(1)}, f32[2,1,4,64,128]{4,3,0,2,1:T(8,128)}, f32[2,1,4,64,128]{4,3,2,1,0:T(8,128)}, f32[2,1,4,64,...) while((s32[]{:T(128)}, ...), condition=%wide.region_37.42_spmd.clone, body=%wide.region_35.41_spmd.clone.sunk | while | flops 706019328 | bytes 25701472 | solution.py:93
  730.6 2.2 fusion.683
  740.0 2.5 fusion.293
  751.6 2.2 fusion.376
  762.4 5.6 multiply_reduce_fusion.3
  777.6 2.4 fusion.278
  781.0 2.2 fusion.172
  785.2 4.5 convolution_convert_fusion.2
  792.1 4.1 copy.594
  796.2 7.3 convolution_convert_fusion
  803.8 5.7 convolution_convert_fusion.1
  809.5 48.0 %concatenate.48 = bf16[1024,12554]{1,0:T(8,128)(2,1)} concatenate(bf16[1024,3072]{1,0:T(8,128)(2,1)} %convolution_convert_fusion.2, bf16[1024,8]{1,0:T(8,128)(2,1)S(1)} %copy.593, bf16[1024,1024]{1,0:T(8,128)(2,1)S(1)} %copy-done.42, bf16[1024,5632]{1,0:T(8,128)(2,1)} %convolution_convert_fusion, bf16[1024,2816]{1,0:T(8,128)(2,1)} %convolution_convert_fusion.1, ...), dimensions={1} | concatenate | bytes 51421184 | tf_op jit(solution)/shard_map/concatenate | solution.py:233
  857.5 427.1 %reduce-scatter.2.cloned.1.call-done = bf16[256,12554]{1,0:T(8,128)(2,1)} async-done(((bf16[1024,12554]{1,0:T(8,128)(2,1)}), bf16[256,12554]{1,0:T(8,128)(2,1)}) %reduce-scatter.2.cloned.1.call-update) | async-done | bytes 6427664 | tf_op jit(solution)/shard_map/reduce_scatter | solution.py:331
  1285.9 5.3 fusion.264
  1291.4 79.9 %all-reduce.51 = (f32[1,4,2048]{2,1,0:T(4,128)}, f32[1,2,4]{2,1,0:T(2,128)}, f32[1,256]{1,0:T(1,128)}) all-reduce(f32[1,4,2048]{2,1,0:T(4,128)S(1)} %add_bitcast_fusion.2, f32[1,2,4]{2,1,0:T(2,128)S(1)} %add_bitcast_fusion.3, f32[1,256]{1,0:T(1,128)S(1)} %bitcast.1621), channel_id=1, replica_groups=mesh['section'=2,'fsdp'=4,'dp'=4] {'fsdp','dp'}, use_global_device_ids=true, to_apply=%region_64.69 | all-reduce | flops 8456 | bytes 67648 | tf_op jit(solution)/shard_map/psum | solution.py:338
  1371.3 62.2 %all-reduce.54.cloned.1.call-done = bf16[256,12554]{1,0:T(8,128)(2,1)} async-done(((bf16[256,12554]{1,0:T(8,128)(2,1)}), bf16[256,12554]{1,0:T(8,128)(2,1)}) %all-reduce.54.cloned.1.call-update) | async-done | bytes 6427664 | tf_op jit(solution)/shard_map/psum | solution.py:337
  1433.5 3.7 convert_element_type.239
  1440.6 4.1 slice_bitcast_fusion
  1444.7 2.4 slice_bitcast_fusion.2
  (1030 shorter events, 232.9 us)
Async XLA Ops:
  7.2 120.7 %all-gather.11.cloned.1.call-start = ((), (), s32[]{:S(2)}) async-start(), calls=%async_computation.3 | async-start | bytes 7864320 | tf_op jit(solution)/shard_map/all_gather | solution.py:280
  7.9 191.2 %all-gather.13.cloned.1.call-start = ((), (), s32[]{:S(2)}) async-start(), calls=%async_computation.4 | async-start | bytes 2621440 | tf_op jit(solution)/shard_map/all_gather | solution.py:282
  8.7 14.3 copy-start.17
  8.7 14.5 copy-start.258
  8.7 31.9 %copy-start.193 = (f32[1,4,2048]{2,1,0:T(4,128)S(1)}, f32[1,4,2048]{2,1,0:T(4,128)}, u32[]{:S(2)}) copy-start(f32[1,4,2048]{2,1,0:T(4,128)} %param.36) | copy-start | bytes 98308
  8.7 366.1 %all-gather.15.cloned.1.call-start = ((), (), s32[]{:S(2)}) async-start(), calls=%async_computation.5 | async-start | bytes 14417920 | tf_op jit(solution)/shard_map/all_gather | solution.py:283
  9.5 471.7 %all-gather.17.cloned.1.call-start = ((), (), s32[]{:S(2)}) async-start(), calls=%async_computation.6 | async-start | bytes 7208960 | tf_op jit(solution)/shard_map/all_gather | solution.py:284
  10.0 1274.6 %reduce-scatter.2.cloned.1.call-start = ((), (), s32[]{:S(2)}) async-start(), calls=%async_computation.1 | async-start | bytes 32440320 | tf_op jit(solution)/shard_map/reduce_scatter | solution.py:331
  10.1 130.4 %copy-start.154 = (f32[64,64]{1,0:T(8,128)}, f32[64,64]{1,0:T(8,128)S(1)}, u32[]{:S(2)}) copy-start(f32[64,64]{1,0:T(8,128)S(1)} %get-tuple-element.1668) | copy-start | bytes 49156
  10.1 130.4 %copy-start.161 = (pred[64,64]{1,0:T(8,128)(4,1)}, pred[64,64]{1,0:T(8,128)(4,1)S(1)}, u32[]{:S(2)}) copy-start(pred[64,64]{1,0:T(8,128)(4,1)S(1)} %get-tuple-element.1667) | copy-start | bytes 12292
  10.2 27.8 %copy-start.233 = (f32[4]{0:T(128)}, f32[4]{0:T(128)S(1)}, u32[]{:S(2)}) copy-start(f32[4]{0:T(128)S(1)} %get-tuple-element.1644) | copy-start | bytes 52
  10.2 30.3 %copy-start.235 = (f32[4]{0:T(128)}, f32[4]{0:T(128)S(1)}, u32[]{:S(2)}) copy-start(f32[4]{0:T(128)S(1)} %get-tuple-element.1645) | copy-start | bytes 52
  10.3 30.2 %copy-start.237 = (pred[128]{0:T(512)(128)(4,1)}, pred[128]{0:T(512)(128)(4,1)S(1)}, u32[]{:S(2)}) copy-start(pred[128]{0:T(512)(128)(4,1)S(1)} %get-tuple-element.1643) | copy-start | bytes 388
  10.3 121.5 %copy-start.198 = (pred[128]{0:T(512)(128)(4,1)}, pred[128]{0:T(512)(128)(4,1)S(1)}, u32[]{:S(2)}) copy-start(pred[128]{0:T(512)(128)(4,1)S(1)} %get-tuple-element.1642) | copy-start | bytes 388
  10.3 121.5 %copy-start.202 = (pred[128]{0:T(512)(128)(4,1)}, pred[128]{0:T(512)(128)(4,1)S(1)}, u32[]{:S(2)}) copy-start(pred[128]{0:T(512)(128)(4,1)S(1)} %get-tuple-element.1646) | copy-start | bytes 388
  10.3 121.5 %copy-start.206 = (pred[128]{0:T(512)(128)(4,1)}, pred[128]{0:T(512)(128)(4,1)S(1)}, u32[]{:S(2)}) copy-start(pred[128]{0:T(512)(128)(4,1)S(1)} %get-tuple-element.1647) | copy-start | bytes 388
  23.0 351.8 %copy-start.151 = (f32[1,1,1024]{2,1,0:T(1,128)}, f32[1,1,1024]{2,1,0:T(1,128)S(1)}, u32[]{:S(2)}) copy-start(f32[1,1,1024]{2,1,0:T(1,128)S(1)} %get-tuple-element.1629) | copy-start | bytes 12292
  23.0 468.9 %copy-start.149 = (f32[1,1,1024]{2,1,0:T(1,128)}, f32[1,1,1024]{2,1,0:T(1,128)S(1)}, u32[]{:S(2)}) copy-start(f32[1,1,1024]{2,1,0:T(1,128)S(1)} %get-tuple-element.1630) | copy-start | bytes 12292
  23.1 14.0 copy-start.271
  23.2 108.5 %copy-start.239 = (f32[128]{0:T(128)}, f32[128]{0:T(128)S(1)}, u32[]{:S(2)}) copy-start(f32[128]{0:T(128)S(1)} %fusion.515) | copy-start | bytes 1540
  36.9 455.1 %copy-start.159 = (bf16[1,1024,8]{1,2,0:T(8,128)(2,1)}, bf16[1,1024,8]{1,2,0:T(8,128)(2,1)S(1)}, u32[]{:S(2)}) copy-start(bf16[1,1024,8]{1,2,0:T(8,128)(2,1)S(1)} %all-gather.1) | copy-start | bytes 49156
  40.5 97.1 %copy-start.177 = (f32[4,2,64]{2,1,0:T(2,128)}, f32[4,2,64]{2,1,0:T(2,128)S(1)}, u32[]{:S(2)}) copy-start(f32[4,2,64]{2,1,0:T(2,128)S(1)} %get-tuple-element.1632) | copy-start | bytes 6148
  40.5 97.1 %copy-start.181 = (f32[4,2,64]{2,1,0:T(2,128)}, f32[4,2,64]{2,1,0:T(2,128)S(1)}, u32[]{:S(2)}) copy-start(f32[4,2,64]{2,1,0:T(2,128)S(1)} %get-tuple-element.1633) | copy-start | bytes 6148
  40.6 140.2 %copy-start.155 = (f32[4,2,64]{2,1,0:T(2,128)}, f32[4,2,64]{2,1,0:T(2,128)S(1)}, u32[]{:S(2)}) copy-start(f32[4,2,64]{2,1,0:T(2,128)S(1)} %mul.1564) | copy-start | bytes 6148
  40.6 91.2 %copy-start.164 = (f32[1,1,2048]{2,1,0:T(1,128)}, f32[1,1,2048]{2,1,0:T(1,128)S(1)}, u32[]{:S(2)}) copy-start(f32[1,1,2048]{2,1,0:T(1,128)S(1)} %get-tuple-element.1618) | copy-start | bytes 24580
  40.6 91.2 %copy-start.167 = (f32[1,1,2048]{2,1,0:T(1,128)}, f32[1,1,2048]{2,1,0:T(1,128)S(1)}, u32[]{:S(2)}) copy-start(f32[1,1,2048]{2,1,0:T(1,128)S(1)} %get-tuple-element.1619) | copy-start | bytes 24580
  40.6 91.2 %copy-start.170 = (f32[1,1,2048]{2,1,0:T(1,128)}, f32[1,1,2048]{2,1,0:T(1,128)S(1)}, u32[]{:S(2)}) copy-start(f32[1,1,2048]{2,1,0:T(1,128)S(1)} %get-tuple-element.1620) | copy-start | bytes 24580
  40.7 91.2 %copy-start.173 = (f32[1,1,2048]{2,1,0:T(1,128)}, f32[1,1,2048]{2,1,0:T(1,128)S(1)}, u32[]{:S(2)}) copy-start(f32[1,1,2048]{2,1,0:T(1,128)S(1)} %get-tuple-element.1621) | copy-start | bytes 24580
  137.4 44.5 %copy-start.59 = (f32[1,4,128,128]{3,1,2,0:T(4,128)}, f32[1,4,128,128]{3,1,2,0:T(4,128)S(1)}, u32[]{:S(2)}) copy-start(f32[1,4,128,128]{3,1,2,0:T(4,128)S(1)} %get-tuple-element.1663) | copy-start | bytes 786436
  139.9 41.1 %copy-start.80 = (f32[1,128,4,256]{3,2,1,0:T(4,128)}, f32[1,128,4,256]{3,2,1,0:T(4,128)S(1)}, u32[]{:S(2)}) copy-start(f32[1,128,4,256]{3,2,1,0:T(4,128)S(1)} %reshape.2328) | copy-start | bytes 1572868
  140.5 40.4 %copy-start.110 = (f32[4,2,64,64]{3,2,1,0:T(8,128)}, f32[4,2,64,64]{3,2,1,0:T(8,128)S(1)}, u32[]{:S(2)}) copy-start(f32[4,2,64,64]{3,2,1,0:T(8,128)S(1)} %fusion.360) | copy-start | bytes 393220
  185.2 10.1 copy-start.189
  192.3 9.4 copy-start.7
  201.8 179.1 %copy-start.275 = (f32[128]{0:T(128)}, f32[128]{0:T(128)S(1)}, u32[]{:S(2)}) copy-start(f32[128]{0:T(128)S(1)} %get-tuple-element.1648) | copy-start | bytes 1540
  201.8 279.4 %copy-start.2 = (f32[128,1024]{1,0:T(8,128)}, f32[128,1024]{1,0:T(8,128)S(1)}, u32[]{:S(2)}) copy-start(f32[128,1024]{1,0:T(8,128)S(1)} %get-tuple-element.1649) | copy-start | bytes 1572868
  201.8 179.0 %copy-start.241 = (f32[128]{0:T(128)}, f32[128]{0:T(128)S(1)}, u32[]{:S(2)}) copy-start(f32[128]{0:T(128)S(1)} %fusion.516) | copy-start | bytes 1540
  382.8 103.0 %copy-start.68 = (bf16[1,128,2816]{2,1,0:T(8,128)(2,1)}, bf16[1,128,2816]{2,1,0:T(8,128)(2,1)S(1)}, u32[]{:S(2)}) copy-start(bf16[1,128,2816]{2,1,0:T(8,128)(2,1)S(1)} %multiply_convert_fusion.1) | copy-start | bytes 2162692
  485.8 5.9 collective-permute-start
  506.8 64.0 %copy-start = (f32[1,4,128,128]{3,1,2,0:T(4,128)}, f32[1,4,128,128]{3,1,2,0:T(4,128)S(1)}, u32[]{:S(2)}) copy-start(f32[1,4,128,128]{3,1,2,0:T(4,128)S(1)} %bitcast_multiply_fusion.30) | copy-start | bytes 786436
  508.6 49.6 %copy-start.55 = (f32[1,4,128,128]{3,1,2,0:T(4,128)}, f32[1,4,128,128]{3,1,2,0:T(4,128)S(1)}, u32[]{:S(2)}) copy-start(f32[1,4,128,128]{3,1,2,0:T(4,128)S(1)} %fusion.391) | copy-start | bytes 786436
  514.0 44.2 %copy-start.114 = (f32[4,2,64,64]{3,2,1,0:T(8,128)}, f32[4,2,64,64]{3,2,1,0:T(8,128)S(1)}, u32[]{:S(2)}) copy-start(f32[4,2,64,64]{3,2,1,0:T(8,128)S(1)} %fusion.357) | copy-start | bytes 393220
  599.6 13.3 copy-start.12
  655.3 12.3 copy-start.109
  658.2 13.3 copy-start.100
  681.1 11.8 slice-start.6
  697.8 4.6 collective-permute-start.1
  768.1 12.1 slice-start.8
  857.5 576.0 %all-reduce.54.cloned.1.call-start = ((), (), s32[]{:S(2)}) async-start(), calls=%async_computation.2 | async-start | bytes 12976128 | tf_op jit(solution)/shard_map/psum | solution.py:337
  (296 other events, 1061.6 us)
Sparse Core Ops, SparseCore 0:
  9.6 118.2 all-gather.10
  129.4 44.0 all-gather.12
  175.1 199.6 all-gather.14
  376.2 104.9 all-gather.16
  857.6 426.9 reduce-scatter.1
  1287.8 145.6 all-reduce.53
where the time goes:
time: 1470 us; the launch traced here: 1460 us
  waiting for transfers between devices  850 us (58%)
  other arithmetic  163 us (11%)
  local copies, waits for them, and re-layouts  161 us (11%)
  matrix products  151 us (10%)
  blocking collectives  106 us (7%)
  between operations  17.9 us (1%)
    reduce_scatter x1, waiting for transfers between devices, shards(): lax.psum_scatter(term_of(jnp.int32(0), own_rows * lax.axis_size('fsdp'))....  427 us
    all_gather x1, waiting for transfers between devices, shards(): lax.all_gather(up_weight[0], 'fsdp', axis=0, tiled=True)  173 us
    all_gather x1, waiting for transfers between devices, shards(): lax.all_gather(down_weight[0], 'fsdp', axis=0, tiled=True)  98.3 us
    all_gather x1, waiting for transfers between devices, shards(): lax.all_gather(proj_weight[0], 'fsdp', axis=0, tiled=True)  86.5 us
    another operation x6, other arithmetic, delta_rule(): lax.linalg.triangular_solve(system, right_side, left_side=True, lower=Tru...  83.3 us
    psum x1, blocking collectives, shards(): lax.psum((small_sum[0], small_sum[1], small_sum[2]), ('fsdp', 'dp'))  79.9 us
    psum x1, waiting for transfers between devices, shards(): totals = lax.psum(totals.astype(jnp.bfloat16), 'dp').astype(jnp.float32)  62.2 us
    concatenate x1, local copies, waits for them, and re-layouts, weight_terms(): jnp.concatenate([product(hidden_one, proj_cot), product(hidden_one, rate_...  48 us
  transfers between devices with their start and end apart: 8, of which 5 were waited for; matrix products, arithmetic and copies ran while one was open for 6% of the time, Pallas kernels for 0%

commit v1 on v0

--- a/solution.py
+++ b/solution.py
@@ -7,6 +7,27 @@
 SPAN = 64
 highest = lax.Precision.HIGHEST
 reset_level = -30.0
+
+
+def ring_gather(x, axis, dim):
+    size, place, rows = (lax.axis_size(axis), lax.axis_index(axis), x.shape[dim])
+    ahead = [(i, (i + 1) % size) for i in range(size)]
+    left = [(i, (i - 1) % size) for i in range(size)]
+    out = jnp.zeros((*x.shape[:dim], size * rows, *x.shape[dim + 1 :]), x.dtype)
+    out = lax.dynamic_update_slice_in_dim(out, x, place * rows, axis=dim)
+    from_left = from_right = x
+    half = size // 2
+    for step in range(1, half + 1):
+        from_left = lax.ppermute(from_left, axis, ahead)
+        out = lax.dynamic_update_slice_in_dim(
+            out, from_left, (place - step) % size * rows, axis=dim
+        )
+        if step < size - half:
+            from_right = lax.ppermute(from_right, axis, left)
+            out = lax.dynamic_update_slice_in_dim(
+                out, from_right, (place + step) % size * rows, axis=dim
+            )
+    return out
 
 
 def passed_along(value, axis, steps):
@@ -277,7 +298,7 @@
     first_section = lax.axis_index("section") == 0
     weights = (
         lax.all_gather(norm_gains[0], "fsdp", axis=1, tiled=True),
-        lax.all_gather(proj_weight[0], "fsdp", axis=0, tiled=True),
+        ring_gather(proj_weight[0], "fsdp", 0),
         lax.all_gather(rate_weight[0], "fsdp", axis=0, tiled=True),
         lax.all_gather(out_weight[0], "fsdp", axis=0, tiled=True),
         lax.all_gather(up_weight[0], "fsdp", axis=0, tiled=True),

time: 1470 us -> 1410 us (0.959)
  waiting for transfers between devices: 850 us -> 691 us
  blocking collectives: 106 us -> 216 us
    all_gather x1, waiting for transfers between devices: 173 us -> 36.2 us  [shards(): lax.all_gather(up_weight[0], 'fsdp', axis=0, tiled=True)]
    all_gather x1, blocking collectives: 12.7 us -> 109 us  [shards(): lax.all_gather(norm_gains[0], 'fsdp', axis=1, tiled=True)]
    all_gather x1 -> x0, waiting for transfers between devices: 86.5 us -> none  [shards(): lax.all_gather(proj_weight[0], 'fsdp', axis=0, tiled=True)]
    ppermute x0 -> x3, waiting for transfers between devices: none -> 65 us  [the longest x2 65 us: ring_gather(): from_left = lax.ppermute(from_left, axis, ahead)]
  transfers between devices with their start and end apart: 8 -> 10, of which waited for: 5 -> 5; matrix products, arithmetic and copies ran while one was open for 6% -> 7% of each run, Pallas kernels for 0% -> 0%
where the time goes in v1:
time: 1410 us; the launch traced here: 1400 us
  waiting for transfers between devices  691 us (49%)
  blocking collectives  216 us (15%)
  local copies, waits for them, and re-layouts  167 us (12%)
  other arithmetic  151 us (11%)
  matrix products  149 us (11%)
  between operations  17.5 us (1%)
    reduce_scatter x1, waiting for transfers between devices, shards(): lax.psum_scatter(term_of(jnp.int32(0), own_rows * lax.axis_size('fsdp'))....  427 us
    all_gather x1, blocking collectives, shards(): lax.all_gather(norm_gains[0], 'fsdp', axis=1, tiled=True)  109 us
    all_gather x1, waiting for transfers between devices, shards(): lax.all_gather(down_weight[0], 'fsdp', axis=0, tiled=True)  99.4 us
    another operation x6, other arithmetic, delta_rule(): lax.linalg.triangular_solve(system, right_side, left_side=True, lower=Tru...  83.2 us
    psum x1, blocking collectives, shards(): lax.psum((small_sum[0], small_sum[1], small_sum[2]), ('fsdp', 'dp'))  79.6 us
    ppermute x2, waiting for transfers between devices, ring_gather(): from_left = lax.ppermute(from_left, axis, ahead)  65 us
    psum x1, waiting for transfers between devices, shards(): totals = lax.psum(totals.astype(jnp.bfloat16), 'dp').astype(jnp.float32)  62.4 us
    concatenate x1, local copies, waits for them, and re-layouts, weight_terms(): jnp.concatenate([product(hidden_one, proj_cot), product(hidden_one, rate_...  47.9 us
  transfers between devices with their start and end apart: 10, of which 5 were waited for; matrix products, arithmetic and copies ran while one was open for 7% of the time, Pallas kernels for 0%

profile of v1, /device:TPU:0, one launch (start us, length us, event | category | flops | bytes accessed | tf_op | source)
XLA Modules:
  0.0 1403.8 jit_solution(12241585020248413162)
XLA Ops:
  8.8 3.1 collective-permute-start
  11.9 2.1 collective-permute-start.1
  14.3 109.1 %all-gather = bf16[1,2,1024]{2,1,0:T(2,128)(2,1)S(1)} all-gather(bf16[1,2,256]{2,1,0:T(2,128)(2,1)S(1)} %copy-done.258), channel_id=2, replica_groups=mesh['section'=2,'fsdp'=4,'dp'=4] {'fsdp'}, dimensions={2}, use_global_device_ids=true | all-gather | bytes 5120 | tf_op jit(solution)/shard_map/all_gather | solution.py:300
  123.6 27.2 %all-gather.1 = bf16[1,1024,8]{1,2,0:T(8,128)(2,1)S(1)} all-gather(bf16[1,256,8]{1,2,0:T(8,128)(2,1)S(1)} %copy-done.247), channel_id=3, replica_groups=mesh['section'=2,'fsdp'=4,'dp'=4] {'fsdp'}, dimensions={1}, use_global_device_ids=true | all-gather | bytes 20480 | tf_op jit(solution)/shard_map/all_gather | solution.py:302
  160.7 65.0 %collective-permute-done.2 = bf16[256,3072]{1,0:T(8,128)(2,1)S(1)} collective-permute-done((bf16[256,3072]{1,0:T(8,128)(2,1)}, bf16[256,3072]{1,0:T(8,128)(2,1)S(1)}, u32[]{:S(2)}, u32[]{:S(2)}) %collective-permute-start.2) | collective-permute-done | bytes 1572896 | tf_op jit(solution)/shard_map/ppermute | solution.py:21
  239.1 39.9 %custom-call.16 = f32[1,4,2,1,64,64]{4,5,3,2,1,0:T(8,128)S(1)} custom-call(f32[1,4,2,1,64,64]{5,4,3,2,1,0:T(8,128)S(1)} %fusion.395), custom_call_target="InvertDiagBlocksLowerTriangular" | custom-call | tf_op jit(solution)/shard_map/jvp()/triangular_solve/custom-call.1 | solution.py:86
  283.4 6.8 while.96
  297.1 2.6 multiply_reduce_fusion.16
  299.8 36.2 %all-gather.11.cloned.1.call-done = bf16[1,1024,5632]{2,1,0:T(8,128)(2,1)} async-done(((bf16[1,256,5632]{2,1,0:T(8,128)(2,1)}), bf16[1,1024,5632]{2,1,0:T(8,128)(2,1)}) %all-gather.11.cloned.1.call-update) | async-done | bytes 11534352 | tf_op jit(solution)/shard_map/all_gather | solution.py:304
  336.0 6.0 fusion.166
  344.0 99.4 %all-gather.13.cloned.1.call-done = bf16[1,1024,2816]{2,1,0:T(8,128)(2,1)} async-done(((bf16[1,256,2816]{2,1,0:T(8,128)(2,1)}), bf16[1,1024,2816]{2,1,0:T(8,128)(2,1)}) %all-gather.13.cloned.1.call-update) | async-done | bytes 5767184 | tf_op jit(solution)/shard_map/all_gather | solution.py:305
  443.4 4.6 fusion.228
  450.0 4.1 copy.525
  455.5 3.8 convolution_bitcast_fusion.16
  470.8 2.2 reshape.2341
  478.0 40.7 %custom-call.17 = f32[1,4,2,1,64,64]{4,5,3,2,1,0:T(8,128)} custom-call(f32[1,4,2,1,64,64]{5,4,3,2,1,0:T(8,128)} %fusion.383), custom_call_target="InvertDiagBlocksLowerTriangular" | custom-call | tf_op jit(solution)/shard_map/jvp()/triangular_solve/custom-call.1 | solution.py:86
  539.2 11.3 while.97
  559.9 2.7 multiply_reduce_fusion.14
  562.8 6.1 fusion.169
  569.0 2.3 fusion.423
  571.5 4.4 fusion.335
  584.9 26.6 %while.98 = (s32[]{:T(128)}, f32[1,4,128,256]{2,3,1,0:T(8,128)S(1)}, f32[2,1,4,64,128]{4,3,0,2,1:T(8,128)}, f32[2,1,4,64,128]{4,3,2,1,0:T(8,128)}, f32[2,1,4,64,...) while((s32[]{:T(128)}, ...), condition=%wide.region_20.23_spmd.clone, body=%wide.region_18.22_spmd.clone.sunk | while | flops 706019328 | bytes 25702096 | solution.py:114
  589.5 2.1 fusion.654
  602.5 2.1 fusion.654
  611.6 2.1 convolution_bitcast_fusion.19
  648.3 2.9 fusion.292
  656.6 4.9 fusion.422
  662.4 3.7 fusion.158
  675.0 19.0 %while.99 = (s32[]{:T(128)}, f32[1,4,128,256]{2,3,1,0:T(8,128)S(1)}, f32[2,1,4,64,128]{4,3,0,2,1:T(8,128)}, f32[2,1,4,64,128]{4,3,2,1,0:T(8,128)}, f32[2,1,4,64,...) while((s32[]{:T(128)}, ...), condition=%wide.region_37.42_spmd.clone, body=%wide.region_35.41_spmd.clone.sunk | while | flops 706019328 | bytes 25701472 | solution.py:114
  675.6 2.2 fusion.675
  685.0 2.2 fusion.675
  694.0 2.1 convolution_bitcast_fusion.18
  705.0 2.2 reduce_window_sum.43
  717.9 2.2 copy.834
  721.5 5.3 multiply_reduce_fusion.3
  730.1 2.4 fusion.294
  733.9 4.5 convolution_convert_fusion.2
  740.8 4.1 copy.594
  745.0 7.1 convolution_convert_fusion
  752.3 5.9 convolution_convert_fusion.1
  758.2 47.9 %concatenate.48 = bf16[1024,12554]{1,0:T(8,128)(2,1)} concatenate(bf16[1024,3072]{1,0:T(8,128)(2,1)} %convolution_convert_fusion.2, bf16[1024,8]{1,0:T(8,128)(2,1)S(1)} %copy.593, bf16[1024,1024]{1,0:T(8,128)(2,1)S(1)} %copy-done.42, bf16[1024,5632]{1,0:T(8,128)(2,1)} %convolution_convert_fusion, bf16[1024,2816]{1,0:T(8,128)(2,1)} %convolution_convert_fusion.1, ...), dimensions={1} | concatenate | bytes 51421184 | tf_op jit(solution)/shard_map/concatenate | solution.py:254
  806.2 427.1 %reduce-scatter.2.cloned.1.call-done = bf16[256,12554]{1,0:T(8,128)(2,1)} async-done(((bf16[1024,12554]{1,0:T(8,128)(2,1)}), bf16[256,12554]{1,0:T(8,128)(2,1)}) %reduce-scatter.2.cloned.1.call-update) | async-done | bytes 6427664 | tf_op jit(solution)/shard_map/reduce_scatter | solution.py:352
  1234.6 5.3 fusion.250
  1240.1 79.6 %all-reduce.51 = (f32[1,4,2048]{2,1,0:T(4,128)}, f32[1,2,4]{2,1,0:T(2,128)}, f32[1,256]{1,0:T(1,128)}) all-reduce(f32[1,4,2048]{2,1,0:T(4,128)S(1)} %add_bitcast_fusion.2, f32[1,2,4]{2,1,0:T(2,128)S(1)} %add_bitcast_fusion.3, f32[1,256]{1,0:T(1,128)S(1)} %bitcast.1610), channel_id=1, replica_groups=mesh['section'=2,'fsdp'=4,'dp'=4] {'fsdp','dp'}, use_global_device_ids=true, to_apply=%region_64.69 | all-reduce | flops 8456 | bytes 67648 | tf_op jit(solution)/shard_map/psum | solution.py:359
  1319.7 62.4 %all-reduce.54.cloned.1.call-done = bf16[256,12554]{1,0:T(8,128)(2,1)} async-done(((bf16[256,12554]{1,0:T(8,128)(2,1)}), bf16[256,12554]{1,0:T(8,128)(2,1)}) %all-reduce.54.cloned.1.call-update) | async-done | bytes 6427664 | tf_op jit(solution)/shard_map/psum | solution.py:358
  1382.1 3.7 convert_element_type.239
  1389.3 4.1 slice_bitcast_fusion
  1393.4 2.4 slice_bitcast_fusion.2
  (1020 shorter events, 232.4 us)
Async XLA Ops:
  7.2 289.9 %all-gather.9.cloned.1.call-start = ((), (), s32[]{:S(2)}) async-start(), calls=%async_computation.3 | async-start | bytes 2621440 | tf_op jit(solution)/shard_map/all_gather | solution.py:303
  7.9 115.5 %copy-start.19 = (bf16[1,1,128,1024]{3,2,1,0:T(8,128)(2,1)S(1)}, bf16[1,1,128,1024]{3,2,1,0:T(8,128)(2,1)}, u32[]{:S(2)}) copy-start(bf16[1,1,128,1024]{3,2,1,0:T(8,128)(2,1)} %param.27) | copy-start | bytes 786436
  8.0 115.6 %copy-start.247 = (bf16[1,256,8]{1,2,0:T(8,128)(2,1)S(1)}, bf16[1,256,8]{1,2,0:T(8,128)(2,1)}, u32[]{:S(2)}) copy-start(bf16[1,256,8]{1,2,0:T(8,128)(2,1)} %param.32) | copy-start | bytes 12292
  8.0 145.8 %copy-start.188 = (f32[1,4,2048]{2,1,0:T(4,128)S(1)}, f32[1,4,2048]{2,1,0:T(4,128)}, u32[]{:S(2)}) copy-start(f32[1,4,2048]{2,1,0:T(4,128)} %param.36) | copy-start | bytes 98308
  8.0 328.0 %all-gather.11.cloned.1.call-start = ((), (), s32[]{:S(2)}) async-start(), calls=%async_computation.4 | async-start | bytes 14417920 | tf_op jit(solution)/shard_map/all_gather | solution.py:304
  8.7 434.7 %all-gather.13.cloned.1.call-start = ((), (), s32[]{:S(2)}) async-start(), calls=%async_computation.5 | async-start | bytes 7208960 | tf_op jit(solution)/shard_map/all_gather | solution.py:305
  8.8 145.2 %collective-permute-start = (bf16[256,3072]{1,0:T(8,128)(2,1)}, bf16[256,3072]{1,0:T(8,128)(2,1)}, u32[]{:S(2)}, u32[]{:S(2)}) collective-permute-start(bf16[256,3072]{1,0:T(8,128)(2,1)} %bitcast.12), channel_id=1, source_target_pairs={{0,4},{4,8},{8,12},{12,0},{1,5},{5,9},{9,13},{13,1},{2,6},{6,10},{... | collective-permute-start | bytes 4718600 | tf_op jit(solution)/shard_map/ppermute | solution.py:21
  11.9 147.3 %collective-permute-start.1 = (bf16[256,3072]{1,0:T(8,128)(2,1)}, bf16[256,3072]{1,0:T(8,128)(2,1)}, u32[]{:S(2)}, u32[]{:S(2)}) collective-permute-start(bf16[256,3072]{1,0:T(8,128)(2,1)} %bitcast.12), channel_id=1, source_target_pairs={{0,12},{4,0},{8,4},{12,8},{1,13},{5,1},{9,5},{13,9},{2,14},{6,2},{... | collective-permute-start | bytes 4718600 | tf_op jit(solution)/shard_map/ppermute | solution.py:26
  14.0 1219.3 %reduce-scatter.2.cloned.1.call-start = ((), (), s32[]{:S(2)}) async-start(), calls=%async_computation.1 | async-start | bytes 32440320 | tf_op jit(solution)/shard_map/reduce_scatter | solution.py:352
  14.1 137.1 %copy-start.222 = (f32[4]{0:T(128)}, f32[4]{0:T(128)S(1)}, u32[]{:S(2)}) copy-start(f32[4]{0:T(128)S(1)} %get-tuple-element.1644) | copy-start | bytes 52
  14.1 139.1 %copy-start.224 = (f32[4]{0:T(128)}, f32[4]{0:T(128)S(1)}, u32[]{:S(2)}) copy-start(f32[4]{0:T(128)S(1)} %get-tuple-element.1645) | copy-start | bytes 52
  14.2 139.0 %copy-start.226 = (pred[128]{0:T(512)(128)(4,1)}, pred[128]{0:T(512)(128)(4,1)S(1)}, u32[]{:S(2)}) copy-start(pred[128]{0:T(512)(128)(4,1)S(1)} %get-tuple-element.1643) | copy-start | bytes 388
  14.3 214.3 %copy-start.193 = (pred[128]{0:T(512)(128)(4,1)}, pred[128]{0:T(512)(128)(4,1)S(1)}, u32[]{:S(2)}) copy-start(pred[128]{0:T(512)(128)(4,1)S(1)} %get-tuple-element.1642) | copy-start | bytes 388
  14.3 214.3 %copy-start.197 = (pred[128]{0:T(512)(128)(4,1)}, pred[128]{0:T(512)(128)(4,1)S(1)}, u32[]{:S(2)}) copy-start(pred[128]{0:T(512)(128)(4,1)S(1)} %get-tuple-element.1646) | copy-start | bytes 388
  14.3 214.3 %copy-start.201 = (pred[128]{0:T(512)(128)(4,1)}, pred[128]{0:T(512)(128)(4,1)S(1)}, u32[]{:S(2)}) copy-start(pred[128]{0:T(512)(128)(4,1)S(1)} %get-tuple-element.1647) | copy-start | bytes 388
  123.4 212.6 %copy-start.151 = (f32[1,1,1024]{2,1,0:T(1,128)}, f32[1,1,1024]{2,1,0:T(1,128)S(1)}, u32[]{:S(2)}) copy-start(f32[1,1,1024]{2,1,0:T(1,128)S(1)} %get-tuple-element.1629) | copy-start | bytes 12292
  123.4 330.9 %copy-start.149 = (f32[1,1,1024]{2,1,0:T(1,128)}, f32[1,1,1024]{2,1,0:T(1,128)S(1)}, u32[]{:S(2)}) copy-start(f32[1,1,1024]{2,1,0:T(1,128)S(1)} %get-tuple-element.1630) | copy-start | bytes 12292
  123.6 27.5 %copy-start.262 = (f32[128]{0:T(128)}, f32[128]{0:T(128)S(1)}, u32[]{:S(2)}) copy-start(f32[128]{0:T(128)S(1)} %fusion.295) | copy-start | bytes 1540
  123.6 102.3 %copy-start.228 = (f32[128]{0:T(128)}, f32[128]{0:T(128)S(1)}, u32[]{:S(2)}) copy-start(f32[128]{0:T(128)S(1)} %fusion.503) | copy-start | bytes 1540
  150.8 303.6 %copy-start.159 = (bf16[1,1024,8]{1,2,0:T(8,128)(2,1)}, bf16[1,1024,8]{1,2,0:T(8,128)(2,1)S(1)}, u32[]{:S(2)}) copy-start(bf16[1,1024,8]{1,2,0:T(8,128)(2,1)S(1)} %all-gather.1) | copy-start | bytes 49156
  153.2 125.8 %copy-start.155 = (f32[4,2,64]{2,1,0:T(2,128)}, f32[4,2,64]{2,1,0:T(2,128)S(1)}, u32[]{:S(2)}) copy-start(f32[4,2,64]{2,1,0:T(2,128)S(1)} %mul.1580) | copy-start | bytes 6148
  153.8 80.9 %copy-start.178 = (f32[4,2,64]{2,1,0:T(2,128)}, f32[4,2,64]{2,1,0:T(2,128)S(1)}, u32[]{:S(2)}) copy-start(f32[4,2,64]{2,1,0:T(2,128)S(1)} %get-tuple-element.1632) | copy-start | bytes 6148
  153.8 80.9 %copy-start.181 = (f32[4,2,64]{2,1,0:T(2,128)}, f32[4,2,64]{2,1,0:T(2,128)S(1)}, u32[]{:S(2)}) copy-start(f32[4,2,64]{2,1,0:T(2,128)S(1)} %get-tuple-element.1633) | copy-start | bytes 6148
  153.8 74.8 %copy-start.166 = (f32[1,1,2048]{2,1,0:T(1,128)}, f32[1,1,2048]{2,1,0:T(1,128)S(1)}, u32[]{:S(2)}) copy-start(f32[1,1,2048]{2,1,0:T(1,128)S(1)} %get-tuple-element.1618) | copy-start | bytes 24580
  153.9 74.8 %copy-start.169 = (f32[1,1,2048]{2,1,0:T(1,128)}, f32[1,1,2048]{2,1,0:T(1,128)S(1)}, u32[]{:S(2)}) copy-start(f32[1,1,2048]{2,1,0:T(1,128)S(1)} %get-tuple-element.1619) | copy-start | bytes 24580
  153.9 74.8 %copy-start.172 = (f32[1,1,2048]{2,1,0:T(1,128)}, f32[1,1,2048]{2,1,0:T(1,128)S(1)}, u32[]{:S(2)}) copy-start(f32[1,1,2048]{2,1,0:T(1,128)S(1)} %get-tuple-element.1620) | copy-start | bytes 24580
  153.9 74.8 %copy-start.175 = (f32[1,1,2048]{2,1,0:T(1,128)}, f32[1,1,2048]{2,1,0:T(1,128)S(1)}, u32[]{:S(2)}) copy-start(f32[1,1,2048]{2,1,0:T(1,128)S(1)} %get-tuple-element.1621) | copy-start | bytes 24580
  154.0 83.6 %copy-start.161 = (pred[64,64]{1,0:T(8,128)(4,1)}, pred[64,64]{1,0:T(8,128)(4,1)S(1)}, u32[]{:S(2)}) copy-start(pred[64,64]{1,0:T(8,128)(4,1)S(1)} %get-tuple-element.1665) | copy-start | bytes 12292
  154.0 71.7 %collective-permute-start.2 = (bf16[256,3072]{1,0:T(8,128)(2,1)}, bf16[256,3072]{1,0:T(8,128)(2,1)S(1)}, u32[]{:S(2)}, u32[]{:S(2)}) collective-permute-start(bf16[256,3072]{1,0:T(8,128)(2,1)} %collective-permute-done), channel_id=1, source_target_pairs={{0,4},{4,8},{8,12},{12,0},{1,5},{5,9},{9,13},{13,1},{2,6},{6,10},{... | collective-permute-start | bytes 4718600 | tf_op jit(solution)/shard_map/ppermute | solution.py:21
  155.1 82.5 %copy-start.154 = (f32[64,64]{1,0:T(8,128)}, f32[64,64]{1,0:T(8,128)S(1)}, u32[]{:S(2)}) copy-start(f32[64,64]{1,0:T(8,128)S(1)} %get-tuple-element.1668) | copy-start | bytes 49156
  234.6 45.5 %copy-start.63 = (f32[1,4,128,128]{3,1,2,0:T(4,128)}, f32[1,4,128,128]{3,1,2,0:T(4,128)S(1)}, u32[]{:S(2)}) copy-start(f32[1,4,128,128]{3,1,2,0:T(4,128)S(1)} %get-tuple-element.1663) | copy-start | bytes 786436
  237.0 43.1 %copy-start.81 = (f32[1,128,4,256]{3,2,1,0:T(4,128)}, f32[1,128,4,256]{3,2,1,0:T(4,128)S(1)}, u32[]{:S(2)}) copy-start(f32[1,128,4,256]{3,2,1,0:T(4,128)S(1)} %reshape.2328) | copy-start | bytes 1572868
  283.4 9.9 copy-start.185
  299.8 42.2 %copy-start.266 = (f32[128]{0:T(128)}, f32[128]{0:T(128)S(1)}, u32[]{:S(2)}) copy-start(f32[128]{0:T(128)S(1)} %get-tuple-element.1648) | copy-start | bytes 1540
  299.8 143.7 %copy-start.3 = (f32[128,1024]{1,0:T(8,128)}, f32[128,1024]{1,0:T(8,128)S(1)}, u32[]{:S(2)}) copy-start(f32[128,1024]{1,0:T(8,128)S(1)} %get-tuple-element.1649) | copy-start | bytes 1572868
  299.8 42.2 %copy-start.230 = (f32[128]{0:T(128)}, f32[128]{0:T(128)S(1)}, u32[]{:S(2)}) copy-start(f32[128]{0:T(128)S(1)} %fusion.504) | copy-start | bytes 1540
  344.0 104.0 %copy-start.70 = (bf16[1,128,2816]{2,1,0:T(8,128)(2,1)}, bf16[1,128,2816]{2,1,0:T(8,128)(2,1)S(1)}, u32[]{:S(2)}) copy-start(bf16[1,128,2816]{2,1,0:T(8,128)(2,1)S(1)} %multiply_convert_fusion.1) | copy-start | bytes 2162692
  448.0 6.0 collective-permute-start.3
  469.1 64.9 %copy-start.1 = (f32[1,4,128,128]{3,1,2,0:T(4,128)}, f32[1,4,128,128]{3,1,2,0:T(4,128)S(1)}, u32[]{:S(2)}) copy-start(f32[1,4,128,128]{3,1,2,0:T(4,128)S(1)} %bitcast_multiply_fusion.30) | copy-start | bytes 786436
  470.8 49.6 %copy-start.57 = (f32[1,4,128,128]{3,1,2,0:T(4,128)}, f32[1,4,128,128]{3,1,2,0:T(4,128)S(1)}, u32[]{:S(2)}) copy-start(f32[1,4,128,128]{3,1,2,0:T(4,128)S(1)} %fusion.377) | copy-start | bytes 786436
  476.3 44.2 %copy-start.111 = (f32[4,2,64,64]{3,2,1,0:T(8,128)}, f32[4,2,64,64]{3,2,1,0:T(8,128)S(1)}, u32[]{:S(2)}) copy-start(f32[4,2,64,64]{3,2,1,0:T(8,128)S(1)} %fusion.343) | copy-start | bytes 393220
  562.6 13.3 copy-start.13
  620.2 12.7 copy-start.69
  624.0 13.1 copy-start.143
  652.1 4.4 collective-permute-start.4
  711.6 9.8 copy-start.12
  711.6 9.8 copy-start.23
  806.2 576.0 %all-reduce.54.cloned.1.call-start = ((), (), s32[]{:S(2)}) async-start(), calls=%async_computation.2 | async-start | bytes 12976128 | tf_op jit(solution)/shard_map/psum | solution.py:358
  (289 other events, 1031.8 us)
Sparse Core Ops, SparseCore 0:
  9.6 89.9 all-gather.8
  101.1 234.8 all-gather.10
  337.6 105.8 all-gather.12
  806.3 426.9 reduce-scatter.1
  1236.5 145.6 all-reduce.53
